TPU v7x, 512 devices: a whole 4x4x16 slice. The times are simulated.
512 devices in a mesh: aux: 32 (over z, y_hi), pair: 16 (over x, y_lo, core).
Axes of the slice: x: 4, y: 4 (y_hi: 2, y_lo: 2; y = y_hi * 2 + y_lo), z: 16, core: 2. Of those that a mesh axis runs over, the one named last changes fastest.
Arguments:
- half_ints: bfloat16 [96, 1408, 4096], P('pair', None, 'aux'), may hold values from -0.75 to 0.75
- vir_coeffs: bfloat16 [1408, 1280], P(None, 'aux'), may hold values from -0.15625 to 0.15625
- occ_energy: float32 [96], replicated, may hold values from -2 to -0.3
- vir_energy: float32 [1280], replicated, may hold values from 0.3 to 4
- roster: int32 [32, 2], replicated, may hold values from 0 to 15
Outputs:
- density: bfloat16 [1280, 96, 4096], P('pair', 'aux')
All inputs are finite; a program needn't handle non-finite values.
Results may differ from a plain program's by a relative error of at most 0.0058.
Values may be sent and summed in bfloat16 or wider, within the bound.
A program may use at most 64 MiB of HBM per device.

v0:
```python
import jax
import jax.numpy as jnp
from jax import lax
from jax.sharding import PartitionSpec as P

spin_scale = 1.3


def broadcast(value, axis, source):
    kept = jnp.where(lax.axis_index(axis) == source, value, 0).astype(value.dtype)
    return lax.psum(kept, axis)


def per_device(half_ints, vir_coeffs, occ_energy, vir_energy, roster):
    occ_rows = half_ints.shape[0]
    aux_slice = half_ints.shape[2]
    half_flat = jnp.transpose(half_ints, (1, 0, 2)).reshape(
        half_ints.shape[1], occ_rows * aux_slice
    )
    columns = lax.all_gather(vir_coeffs, "aux", axis=1, tiled=True)
    product = jnp.dot(jnp.transpose(columns), half_flat, preferred_element_type=jnp.float32)
    vir_ints = product.astype(jnp.bfloat16).reshape(columns.shape[1], occ_rows, aux_slice)
    by_virtual = lax.all_to_all(vir_ints, "pair", split_axis=0, concat_axis=1, tiled=True)
    aux_count = lax.axis_size("aux")
    aux_index = lax.axis_index("aux")
    pair_index = lax.axis_index("pair")
    vir_width = by_virtual.shape[0]
    occ_width = by_virtual.shape[1] // aux_count
    step_count = roster.shape[1]
    block_plan = lax.dynamic_index_in_dim(roster, aux_index, 0, keepdims=False)
    sources = []
    for position in range(step_count):
        sources.append(lax.dynamic_index_in_dim(block_plan, position, 0, keepdims=False))
    own_block = lax.all_to_all(by_virtual, "aux", split_axis=1, concat_axis=2, tiled=True)
    remotes = [broadcast(own_block, "pair", source) for source in sources]
    aux_total = own_block.shape[2]
    flat_local = own_block.reshape(vir_width * occ_width, aux_total)
    occ_block = lax.dynamic_slice_in_dim(occ_energy, aux_index * occ_width, occ_width, 0)
    vir_block = lax.dynamic_slice_in_dim(vir_energy, pair_index * vir_width, vir_width, 0)
    energy_left = (vir_block[:, None] - occ_block[None, :]).reshape(-1)
    density = jnp.zeros((vir_width * occ_width, aux_total), jnp.float32)
    for position in range(step_count):
        flat_remote = remotes[position].reshape(vir_width * occ_width, aux_total)
        energy_block = lax.dynamic_slice_in_dim(
            vir_energy, sources[position] * vir_width, vir_width, 0
        )
        energy_right = (energy_block[:, None] - occ_block[None, :]).reshape(-1)
        integrals = jnp.dot(
            flat_local, jnp.transpose(flat_remote), preferred_element_type=jnp.float32
        )
        amplitudes = (
            spin_scale * integrals / (energy_left[:, None] + energy_right[None, :])
        ).astype(jnp.bfloat16)
        density = density + jnp.dot(amplitudes, flat_remote, preferred_element_type=jnp.float32)
    return density.astype(jnp.bfloat16).reshape(vir_width, occ_width, aux_total)


def solution(mesh):
    in_specs = (P("pair", None, "aux"), P(None, "aux"), P(), P(), P())
    out_specs = P("pair", "aux", None)
    return jax.shard_map(
        per_device, mesh=mesh, in_specs=in_specs, out_specs=out_specs, check_vma=False
    )
```

profile of v0, /device:TPU:15, one launch (start us, length us, event | category | flops | bytes accessed | tf_op | source)
XLA Modules:
  0.0 497.1 jit_solution(2042534354434699088)
XLA Ops:
  6.5 0.7 all-gather.2.cloned.1.call-update
  7.3 2.9 copy.14
  10.2 153.8 %all-gather.2.cloned.1.call-done = bf16[1408,1280]{0,1:T(8,128)(2,1)} async-done(((bf16[1408,40]{0,1:T(8,128)(2,1)}), bf16[1408,1280]{0,1:T(8,128)(2,1)}) %all-gather.2.cloned.1.call-update) | async-done | bytes 3604496 | tf_op jit(solution)/shard_map/all_gather | solution.py:20
  164.0 6.4 %convolution_convert_fusion = bf16[1280,768]{0,1:T(8,128)(2,1)} fusion(bf16[1408,1280]{0,1:T(8,128)(2,1)} %all-gather.2.cloned.1.call-done, bf16[1408,768]{0,1:T(8,128)(2,1)S(1)} %bitcast.58), kind=kOutput, calls=%fused_computation.2 | convolution fusion | flops 2769223680 | bytes 7733248 | tf_op jit(solution)/shard_map/dot_general | solution.py:21
  170.4 3.9 copy.15
  174.3 45.4 %all_to_all.33 = bf16[1280,6,128]{2,1,0:T(8,128)(2,1)S(1)} all-to-all(bf16[1280,6,128]{2,1,0:T(8,128)(2,1)S(1)} %copy.15), channel_id=1, replica_groups=mesh['aux'=32,'pair'=16] {'pair'}, dimensions={0} | all-to-all | bytes 3932160 | tf_op jit(solution)/shard_map/all_to_all | solution.py:23
  219.7 1.5 copy.17
  221.2 7.8 %all-to-all-start.1 = ((bf16[80,96,128]{2,0,1:T(8,128)(2,1)}), bf16[80,96,128]{2,0,1:T(8,128)(2,1)S(1)}, u32[]{:S(2)}, u32[]{:S(2)}) async-start(bf16[80,96,128]{2,0,1:T(8,128)(2,1)} %bitcast.55), calls=%async_computation.1 | async-start | bytes 3932160 | tf_op jit(solution)/shard_map/all_to_all | solution.py:34
  229.0 0.2 all-reduce.3.cloned.1.call-start
  229.3 0.6 fusion.41
  231.2 89.0 %all-to-all-done.1 = bf16[80,96,128]{2,0,1:T(8,128)(2,1)S(1)} async-done(((bf16[80,96,128]{2,0,1:T(8,128)(2,1)}), bf16[80,96,128]{2,0,1:T(8,128)(2,1)S(1)}, u32[]{:S(2)}, u32[]{:S(2)}) %all-to-all-start.1) | async-done | bytes 1966112 | tf_op jit(solution)/shard_map/all_to_all | solution.py:34
  320.2 0.3 broadcast_select_fusion
  320.4 1.0 copy-done.1
  321.4 0.5 copy.20
  322.0 0.5 copy.19
  322.5 5.2 %copy_bitcast_fusion = (bf16[240,4096]{1,0:T(8,128)(2,1)}, bf16[240,4096]{1,0:T(8,128)(2,1)}) fusion(bf16[30,8,32,128]{3,2,1,0:T(8,128)(2,1)S(1)} %bitcast.56, bf16[30,8,32,128]{3,2,1,0:T(8,128)(2,1)S(1)} %bitcast.57), kind=kLoop, calls=%fused_computation.3 | loop fusion | bytes 7864320 | tf_op jit(solution)/shard_map/reshape | solution.py:43
  329.1 0.9 fusion.40
  330.2 0.2 sub.59
  330.5 2.1 copy.18
  332.6 137.9 %all-reduce.3.cloned.1.call-done = (bf16[240,4096]{1,0:T(8,128)(2,1)}, bf16[240,4096]{1,0:T(8,128)(2,1)}) async-done(((bf16[240,4096]{1,0:T(8,128)(2,1)}, bf16[240,4096]{1,0:T(8,128)(2,1)}), (bf16[240,4096]{1,0:T(8,128)(2,1)}, bf16[240,4096]{1,0:T(8,128)(2,1)})) %all-reduce.3.cloned.1.call-update) | async-done | bytes 3932176 | tf_op jit(solution)/shard_map/psum | solution.py:11
  470.5 6.4 %fusion.26 = f32[240,4096]{1,0:T(8,128)} fusion(bf16[240,4096]{1,0:T(8,128)(2,1)} %get-tuple-element.5, bf16[30,8,32,128]{3,2,1,0:T(8,128)(2,1)S(1)} %bitcast.50, f32[240]{0:T(256)S(1)} %sub.62, f32[240]{0:T(256)S(1)} %sub.59), kind=kOutput, calls=%fused_computation.19 | convolution fusion | flops 943948800 | bytes 7866240 | tf_op jit(solution)/shard_map/dot_general | solution.py:54
  476.8 7.0 %fusion = bf16[240,4096]{1,0:T(8,128)(2,1)} fusion(f32[240,4096]{1,0:T(8,128)} %fusion.26, bf16[240,4096]{1,0:T(8,128)(2,1)} %get-tuple-element.6, bf16[30,8,32,128]{3,2,1,0:T(8,128)(2,1)S(1)} %bitcast.51, f32[240]{0:T(256)S(1)} %sub.65, f32[240]{0:T(256)S(1)} %sub.59), kind=kOutput, calls=%fused_computation.1 | convolution fusion | flops 945914880 | bytes 9832320 | tf_op jit(solution)/shard_map/dot_general | solution.py:54
  483.8 3.7 reshape.80
  487.5 2.7 copy.21
  (12 shorter events, 0.6 us)
Async XLA Ops:
  6.5 222.7 %copy-start = (s32[32,2]{0,1:T(2,128)S(1)}, s32[32,2]{0,1:T(2,128)}, u32[]{:S(2)}) copy-start(s32[32,2]{0,1:T(2,128)} %param.9) | copy-start | bytes 772
  6.5 157.5 %all-gather.2.cloned.1.call-start = ((), (), s32[]{:S(2)}) async-start(), calls=%async_computation.2 | async-start | bytes 3717120 | tf_op jit(solution)/shard_map/all_gather | solution.py:20
  221.2 99.0 %all-to-all-start.1 = ((bf16[80,96,128]{2,0,1:T(8,128)(2,1)}), bf16[80,96,128]{2,0,1:T(8,128)(2,1)S(1)}, u32[]{:S(2)}, u32[]{:S(2)}) async-start(bf16[80,96,128]{2,0,1:T(8,128)(2,1)} %bitcast.55), calls=%async_computation.1 | async-start | bytes 3932160 | tf_op jit(solution)/shard_map/all_to_all | solution.py:34
  229.0 241.4 %all-reduce.3.cloned.1.call-start = ((), (), s32[]{:S(2)}) async-start(), calls=%async_computation.3 | async-start | bytes 7864320 | tf_op jit(solution)/shard_map/psum | solution.py:11
  320.2 1.3 copy-start.1
  327.7 1.3 copy-start.2
Sparse Core Ops, SparseCore 0:
  10.5 153.4 all-gather.1
  327.9 142.5 all-reduce.2
where the time goes:
time: 498 us; the launch traced here: 497 us
  waiting for transfers between devices  381 us (77%)
  blocking collectives  45.4 us (9%)
  local copies, waits for them, and re-layouts  26.1 us (5%)
  matrix products  19.8 us (4%)
  between operations  16 us (3%)
  starting transfers between devices  8.03 us (2%)
    all_gather x1, waiting for transfers between devices, per_device(): columns = lax.all_gather(vir_coeffs, 'aux', axis=1, tiled=True)  154 us
    psum x1, waiting for transfers between devices, broadcast(): return lax.psum(kept, axis)  138 us
    all_to_all x1, waiting for transfers between devices, per_device(): lax.all_to_all(by_virtual, 'aux', split_axis=1, concat_axis=2, tiled=True)  89 us
    all_to_all x1, blocking collectives, per_device(): lax.all_to_all(vir_ints, 'pair', split_axis=0, concat_axis=1, tiled=True)  45.4 us
    dot_general x2, matrix products, per_device(): jnp.dot(amplitudes, flat_remote, preferred_element_type=jnp.float32)  13.3 us
  transfers between devices with their start and end apart: 3, of which 3 were waited for; matrix products, arithmetic and copies ran while one was open for 1% of the time, Pallas kernels for 0%

commit v1 on v0

--- a/solution.py
+++ b/solution.py
@@ -17,7 +17,9 @@
     half_flat = jnp.transpose(half_ints, (1, 0, 2)).reshape(
         half_ints.shape[1], occ_rows * aux_slice
     )
-    columns = lax.all_gather(vir_coeffs, "aux", axis=1, tiled=True)
+    columns = jnp.concatenate(
+        lax.all_to_all(jnp.stack([vir_coeffs] * lax.axis_size("aux")), "aux", 0, 0), axis=1
+    )
     product = jnp.dot(jnp.transpose(columns), half_flat, preferred_element_type=jnp.float32)
     vir_ints = product.astype(jnp.bfloat16).reshape(columns.shape[1], occ_rows, aux_slice)
     by_virtual = lax.all_to_all(vir_ints, "pair", split_axis=0, concat_axis=1, tiled=True)

time: 498 us -> 513 us (1.030)
  starting transfers between devices: 8.03 us -> 27.8 us
  blocking collectives: 45.4 us -> 35.3 us
    all_to_all x0 -> x1, waiting for transfers between devices: none -> 157 us  [per_device(): lax.all_to_all(jnp.stack([vir_coeffs] * lax.axis_size('aux')), 'aux', 0, 0)]
    all_gather x1 -> x0, waiting for transfers between devices: 154 us -> none  [per_device(): columns = lax.all_gather(vir_coeffs, 'aux', axis=1, tiled=True)]
    all_to_all x0 -> x1, starting transfers between devices: none -> 17.2 us  [per_device(): lax.all_to_all(jnp.stack([vir_coeffs] * lax.axis_size('aux')), 'aux', 0, 0)]
    all_to_all x1, blocking collectives: 45.4 us -> 35.3 us  [per_device(): lax.all_to_all(vir_ints, 'pair', split_axis=0, concat_axis=1, tiled=True)]
where the time goes in v1:
time: 513 us
  waiting for transfers between devices  384 us (75%)
  blocking collectives  35.3 us (7%)
  local copies, waits for them, and re-layouts  28.7 us (6%)
  starting transfers between devices  27.8 us (5%)
  matrix products  20.6 us (4%)
  between operations  16 us (3%)
    all_to_all x1, waiting for transfers between devices, per_device(): lax.all_to_all(jnp.stack([vir_coeffs] * lax.axis_size('aux')), 'aux', 0, 0)  157 us
    psum x1, waiting for transfers between devices, broadcast(): return lax.psum(kept, axis)  138 us
    all_to_all x1, waiting for transfers between devices, per_device(): lax.all_to_all(by_virtual, 'aux', split_axis=1, concat_axis=2, tiled=True)  89 us
    all_to_all x1, blocking collectives, per_device(): lax.all_to_all(vir_ints, 'pair', split_axis=0, concat_axis=1, tiled=True)  35.3 us
    all_to_all x1, starting transfers between devices, per_device(): lax.all_to_all(jnp.stack([vir_coeffs] * lax.axis_size('aux')), 'aux', 0, 0)  17.2 us
    dot_general x2, matrix products, per_device(): jnp.dot(amplitudes, flat_remote, preferred_element_type=jnp.float32)  13.3 us
    all_to_all x1, starting transfers between devices, per_device(): lax.all_to_all(by_virtual, 'aux', split_axis=1, concat_axis=2, tiled=True)  10.4 us
  transfers between devices with their start and end apart: 3, of which 3 were waited for; matrix products, arithmetic and copies ran while one was open for 1% of the time, Pallas kernels for 0%

profile of v1, /device:TPU:15, one launch (start us, length us, event | category | flops | bytes accessed | tf_op | source)
XLA Modules:
  0.0 512.6 jit_solution(7878513636239327724)
XLA Ops:
  6.5 3.0 stack.2
  9.5 17.2 %all-to-all-start = ((bf16[32,1408,40]{1,2,0:T(8,128)(2,1)}), bf16[32,1408,40]{1,2,0:T(8,128)(2,1)}, u32[]{:S(2)}, u32[]{:S(2)}) async-start(bf16[32,1408,40]{1,2,0:T(8,128)(2,1)} %stack.2), calls=%async_computation | async-start | bytes 7208960 | tf_op jit(solution)/shard_map/all_to_all | solution.py:21
  26.7 2.5 copy.15
  29.2 157.1 %all-to-all-done = bf16[32,1408,40]{1,2,0:T(8,128)(2,1)} async-done(((bf16[32,1408,40]{1,2,0:T(8,128)(2,1)}), bf16[32,1408,40]{1,2,0:T(8,128)(2,1)}, u32[]{:S(2)}, u32[]{:S(2)}) %all-to-all-start) | async-done | bytes 3604512 | tf_op jit(solution)/shard_map/all_to_all | solution.py:21
  186.3 7.2 %convolution_convert_fusion = bf16[1280,768]{0,1:T(8,128)(2,1)} fusion(bf16[1408,1280]{0,1:T(8,128)(2,1)} %bitcast.1, bf16[1408,768]{0,1:T(8,128)(2,1)} %bitcast.61), kind=kOutput, calls=%fused_computation.2 | convolution fusion | flops 2769223680 | bytes 7733248 | tf_op jit(solution)/shard_map/dot_general | solution.py:23
  193.5 3.9 copy.16
  197.4 35.3 %all_to_all.38 = bf16[1280,6,128]{2,1,0:T(8,128)(2,1)S(1)} all-to-all(bf16[1280,6,128]{2,1,0:T(8,128)(2,1)S(1)} %copy.16), channel_id=1, replica_groups=mesh['aux'=32,'pair'=16] {'pair'}, dimensions={0} | all-to-all | bytes 3932160 | tf_op jit(solution)/shard_map/all_to_all | solution.py:25
  232.7 1.5 copy.18
  234.2 10.4 %all-to-all-start.2 = ((bf16[80,96,128]{2,0,1:T(8,128)(2,1)}), bf16[80,96,128]{2,0,1:T(8,128)(2,1)S(1)}, u32[]{:S(2)}, u32[]{:S(2)}) async-start(bf16[80,96,128]{2,0,1:T(8,128)(2,1)} %bitcast.58), calls=%async_computation.2 | async-start | bytes 3932160 | tf_op jit(solution)/shard_map/all_to_all | solution.py:36
  244.6 0.2 all-reduce.3.cloned.1.call-start
  244.9 0.6 fusion.41
  246.7 89.0 %all-to-all-done.2 = bf16[80,96,128]{2,0,1:T(8,128)(2,1)S(1)} async-done(((bf16[80,96,128]{2,0,1:T(8,128)(2,1)}), bf16[80,96,128]{2,0,1:T(8,128)(2,1)S(1)}, u32[]{:S(2)}, u32[]{:S(2)}) %all-to-all-start.2) | async-done | bytes 1966112 | tf_op jit(solution)/shard_map/all_to_all | solution.py:36
  335.8 0.3 broadcast_select_fusion
  336.0 1.0 copy-done.1
  337.0 0.5 copy.21
  337.5 0.5 copy.20
  338.0 5.2 %copy_bitcast_fusion = (bf16[240,4096]{1,0:T(8,128)(2,1)}, bf16[240,4096]{1,0:T(8,128)(2,1)}) fusion(bf16[30,8,32,128]{3,2,1,0:T(8,128)(2,1)S(1)} %bitcast.59, bf16[30,8,32,128]{3,2,1,0:T(8,128)(2,1)S(1)} %bitcast.60), kind=kLoop, calls=%fused_computation.3 | loop fusion | bytes 7864320 | tf_op jit(solution)/shard_map/reshape | solution.py:45
  344.6 0.9 fusion.40
  346.1 2.1 copy.19
  348.1 137.9 %all-reduce.3.cloned.1.call-done = (bf16[240,4096]{1,0:T(8,128)(2,1)}, bf16[240,4096]{1,0:T(8,128)(2,1)}) async-done(((bf16[240,4096]{1,0:T(8,128)(2,1)}, bf16[240,4096]{1,0:T(8,128)(2,1)}), (bf16[240,4096]{1,0:T(8,128)(2,1)}, bf16[240,4096]{1,0:T(8,128)(2,1)})) %all-reduce.3.cloned.1.call-update) | async-done | bytes 3932176 | tf_op jit(solution)/shard_map/psum | solution.py:11
  486.0 6.4 %fusion.26 = f32[240,4096]{1,0:T(8,128)} fusion(bf16[240,4096]{1,0:T(8,128)(2,1)} %get-tuple-element.5, bf16[30,8,32,128]{3,2,1,0:T(8,128)(2,1)S(1)} %bitcast.53, f32[240]{0:T(256)S(1)} %sub.62, f32[240]{0:T(256)S(1)} %sub.59), kind=kOutput, calls=%fused_computation.19 | convolution fusion | flops 943948800 | bytes 7866240 | tf_op jit(solution)/shard_map/dot_general | solution.py:56
  492.4 7.0 %fusion = bf16[240,4096]{1,0:T(8,128)(2,1)} fusion(f32[240,4096]{1,0:T(8,128)} %fusion.26, bf16[240,4096]{1,0:T(8,128)(2,1)} %get-tuple-element.6, bf16[30,8,32,128]{3,2,1,0:T(8,128)(2,1)S(1)} %bitcast.54, f32[240]{0:T(256)S(1)} %sub.65, f32[240]{0:T(256)S(1)} %sub.59), kind=kOutput, calls=%fused_computation.1 | convolution fusion | flops 945914880 | bytes 9832320 | tf_op jit(solution)/shard_map/dot_general | solution.py:56
  499.4 3.7 reshape.90
  503.1 2.7 copy.22
  (14 shorter events, 0.7 us)
Async XLA Ops:
  6.5 238.3 %copy-start = (s32[32,2]{0,1:T(2,128)S(1)}, s32[32,2]{0,1:T(2,128)}, u32[]{:S(2)}) copy-start(s32[32,2]{0,1:T(2,128)} %param.9) | copy-start | bytes 772
  9.5 17.2 %copy-start.2 = (bf16[6,1408,128]{2,1,0:T(8,128)(2,1)S(1)}, bf16[6,1408,128]{2,1,0:T(8,128)(2,1)}, u32[]{:S(2)}) copy-start(bf16[6,1408,128]{2,1,0:T(8,128)(2,1)} %param.5) | copy-start | bytes 6488068
  9.5 176.8 %all-to-all-start = ((bf16[32,1408,40]{1,2,0:T(8,128)(2,1)}), bf16[32,1408,40]{1,2,0:T(8,128)(2,1)}, u32[]{:S(2)}, u32[]{:S(2)}) async-start(bf16[32,1408,40]{1,2,0:T(8,128)(2,1)} %stack.2), calls=%async_computation | async-start | bytes 7208960 | tf_op jit(solution)/shard_map/all_to_all | solution.py:21
  234.2 101.6 %all-to-all-start.2 = ((bf16[80,96,128]{2,0,1:T(8,128)(2,1)}), bf16[80,96,128]{2,0,1:T(8,128)(2,1)S(1)}, u32[]{:S(2)}, u32[]{:S(2)}) async-start(bf16[80,96,128]{2,0,1:T(8,128)(2,1)} %bitcast.58), calls=%async_computation.2 | async-start | bytes 3932160 | tf_op jit(solution)/shard_map/all_to_all | solution.py:36
  244.6 241.4 %all-reduce.3.cloned.1.call-start = ((), (), s32[]{:S(2)}) async-start(), calls=%async_computation.3 | async-start | bytes 7864320 | tf_op jit(solution)/shard_map/psum | solution.py:11
  335.8 1.3 copy-start.1
  343.3 1.3 copy-start.3
Sparse Core Ops, SparseCore 0:
  343.4 142.5 all-reduce.2
